TPU v7x, 32 devices: a whole 2x2x4 slice. The times are simulated.
32 devices in a mesh: dp: 8 (over z, x), tensor: 4 (over y, core).
Axes of the slice: x: 2, y: 2, z: 4, core: 2. Of those that a mesh axis runs over, the one named last changes fastest.
Arguments:
- block_input: bfloat16 [16384, 768], P(('dp', 'tensor')), may hold values from -6 to 6
- output_grad: bfloat16 [16384, 768], P(('dp', 'tensor')), may hold values from -6 to 6
- lengths: int32 [8], P('dp'), may hold values from 1024 to 2048, as said below
- in_proj: float32 [768, 2, 1536], P('dp', None, 'tensor'), may hold values from -0.21875 to 0.21875
- step_proj: float32 [768, 24], P('dp', 'tensor'), may hold values from -0.21875 to 0.21875
- out_proj: float32 [768, 1536], P('dp', 'tensor'), may hold values from -0.15625 to 0.15625
- channel_params: float32 [6, 1536], P(None, 'tensor'), may hold values from -0.6 to 1.5
- head_params: float32 [3, 24], P(None, 'tensor'), may hold values from -6 to 2.31
- state_proj: float32 [768, 256], P(('dp', 'tensor')), may hold values from -0.21875 to 0.21875
- state_conv: float32 [256, 5], P(('dp', 'tensor')), may hold values from -0.5 to 0.5
- norm_gain: float32 [768], P(('dp', 'tensor')), may hold values from 0.5 to 1.5
- first_in_proj: float32 [768, 2, 1536], P('dp', None, 'tensor'), may hold values from -1200 to 1200
- first_step_proj: float32 [768, 24], P('dp', 'tensor'), may hold values from -1200 to 1200
- first_out_proj: float32 [768, 1536], P('dp', 'tensor'), may hold values from -1200 to 1200
- first_channel_params: float32 [6, 1536], P(None, 'tensor'), may hold values from -1200 to 1200
- first_head_params: float32 [3, 24], P(None, 'tensor'), may hold values from -1200 to 1200
- first_state_proj: float32 [768, 256], P(('dp', 'tensor')), may hold values from -1200 to 1200
- first_state_conv: float32 [256, 5], P(('dp', 'tensor')), may hold values from -1200 to 1200
- first_norm_gain: float32 [768], P(('dp', 'tensor')), may hold values from -1200 to 1200
- second_in_proj: float32 [768, 2, 1536], P('dp', None, 'tensor'), may hold values from 1000 to 100000
- second_step_proj: float32 [768, 24], P('dp', 'tensor'), may hold values from 1000 to 100000
- second_out_proj: float32 [768, 1536], P('dp', 'tensor'), may hold values from 1000 to 100000
- second_channel_params: float32 [6, 1536], P(None, 'tensor'), may hold values from 1000 to 100000
- second_head_params: float32 [3, 24], P(None, 'tensor'), may hold values from 1000 to 100000
- second_state_proj: float32 [768, 256], P(('dp', 'tensor')), may hold values from 1000 to 100000
- second_state_conv: float32 [256, 5], P(('dp', 'tensor')), may hold values from 1000 to 100000
- second_norm_gain: float32 [768], P(('dp', 'tensor')), may hold values from 1000 to 100000
Outputs:
- output: bfloat16 [16384, 768], P(('dp', 'tensor'))
- input_grad: float32 [16384, 768], P(('dp', 'tensor'))
- grad_in_proj: float32 [768, 2, 1536], P('dp', None, 'tensor')
- grad_step_proj: float32 [768, 24], P('dp', 'tensor')
- grad_out_proj: float32 [768, 1536], P('dp', 'tensor')
- grad_channel_params: float32 [6, 1536], P(None, 'tensor')
- grad_head_params: float32 [3, 24], P(None, 'tensor')
- grad_state_proj: float32 [768, 256], P(('dp', 'tensor'))
- grad_state_conv: float32 [256, 5], P(('dp', 'tensor'))
- grad_norm_gain: float32 [768], P(('dp', 'tensor'))
- new_first_in_proj: float32 [768, 2, 1536], P('dp', None, 'tensor')
- new_first_step_proj: float32 [768, 24], P('dp', 'tensor')
- new_first_out_proj: float32 [768, 1536], P('dp', 'tensor')
- new_first_channel_params: float32 [6, 1536], P(None, 'tensor')
- new_first_head_params: float32 [3, 24], P(None, 'tensor')
- new_first_state_proj: float32 [768, 256], P(('dp', 'tensor'))
- new_first_state_conv: float32 [256, 5], P(('dp', 'tensor'))
- new_first_norm_gain: float32 [768], P(('dp', 'tensor'))
- new_second_in_proj: float32 [768, 2, 1536], P('dp', None, 'tensor')
- new_second_step_proj: float32 [768, 24], P('dp', 'tensor')
- new_second_out_proj: float32 [768, 1536], P('dp', 'tensor')
- new_second_channel_params: float32 [6, 1536], P(None, 'tensor')
- new_second_head_params: float32 [3, 24], P(None, 'tensor')
- new_second_state_proj: float32 [768, 256], P(('dp', 'tensor'))
- new_second_state_conv: float32 [256, 5], P(('dp', 'tensor'))
- new_second_norm_gain: float32 [768], P(('dp', 'tensor'))
- update_in_proj: float32 [768, 2, 1536], P('dp', None, 'tensor')
- update_step_proj: float32 [768, 24], P('dp', 'tensor')
- update_out_proj: float32 [768, 1536], P('dp', 'tensor')
- update_channel_params: float32 [6, 1536], P(None, 'tensor')
- update_head_params: float32 [3, 24], P(None, 'tensor')
- update_state_proj: float32 [768, 256], P(('dp', 'tensor'))
- update_state_conv: float32 [256, 5], P(('dp', 'tensor'))
- update_norm_gain: float32 [768], P(('dp', 'tensor'))
- lamb_norms: float32 [2, 8], replicated
Inputs may be any that keep to these rules, and one draw needn't show every extreme that they name: `lengths`: some sequence has exactly 2048 live positions.
All inputs are finite; a program needn't handle non-finite values.
Results may differ from a plain program's by a relative error of at most 0.012.
The roundings to bfloat16 on the way count: a program that leaves them out, or rounds other values in their place, can miss the bound.
Values may be sent and summed in bfloat16 or wider, within the bound.
No kernel may reach another device: no remote copies, remote signals or barrier semaphores. Data moves between devices by JAX's collectives and lax.ppermute only.
A program may use at most 192 MiB of HBM per device.

v0:
```python
import jax
import jax.numpy as jnp
from jax import lax
from jax.sharding import PartitionSpec as P

STATE = 128
CONV = 4
SPAN = 256
LMAX = 2048
INNER = 1536
EPSILON = 1e-05
ADAM_EPSILON = 1e-06
DECAY = 0.5
BIAS_FIRST = 0.875
BIAS_SECOND = 0.875
RATE = 0.3
WEIGHT_DECAY = 0.01
HIGHEST = lax.Precision.HIGHEST


def rounded(values):
    return lax.optimization_barrier(values.astype(jnp.bfloat16)).astype(jnp.float32)


def contract(left, right, left_dim, right_dim):
    return lax.dot_general(
        left, right, (((left_dim,), (right_dim,)), ((), ())), preferred_element_type=jnp.float32
    )


def causal_conv(values, kernel, offsets):
    padded = jnp.pad(values, ((kernel.shape[0] - 1, 0), (0, 0)))
    summed = offsets[None, :] + jnp.zeros_like(values)
    for offset in range(kernel.shape[0]):
        summed = summed + kernel[offset][None, :] * padded[offset : offset + values.shape[0]]
    return jax.nn.silu(summed)


def ssd_scan(signal, b_rows, c_rows, step_size, log_rate):
    length, head_count, head_width = signal.shape
    blocks = length // SPAN
    decay_log = -jnp.exp(log_rate)[None, :] * step_size
    x_blocks = signal.reshape(blocks, SPAN, head_count, head_width)
    dt_blocks = step_size.reshape(blocks, SPAN, head_count)
    b_blocks = b_rows.reshape(blocks, SPAN, -1)
    c_blocks = c_rows.reshape(blocks, SPAN, -1)
    cumulative = jnp.cumsum(decay_log.reshape(blocks, SPAN, head_count), axis=1)
    intersection = jnp.einsum("cqn,ckn->cqk", c_blocks, b_blocks, precision=HIGHEST)
    causal = jnp.arange(SPAN)[:, None] >= jnp.arange(SPAN)[None, :]
    spread = cumulative[:, :, None, :] - cumulative[:, None, :, :]
    damping = jnp.exp(jnp.where(causal[None, :, :, None], spread, -jnp.inf))
    mixing = intersection[:, :, :, None] * damping * dt_blocks[:, None, :, :]
    within = jnp.einsum("cqkh,ckhp->cqhp", mixing, x_blocks, precision=HIGHEST)
    closing = cumulative[:, -1, :]
    weights_end = jnp.exp(closing[:, None, :] - cumulative) * dt_blocks
    states = jnp.einsum("ckh,ckhp,ckn->chpn", weights_end, x_blocks, b_blocks, precision=HIGHEST)

    def carry_step(carried, element):
        state_new, closing_new = element
        return (jnp.exp(closing_new)[:, None, None] * carried + state_new, carried)

    initial = jnp.zeros(states.shape[1:], jnp.float32)
    unused, entering = lax.scan(carry_step, initial, (states, closing))
    across = (
        jnp.einsum("cqn,chpn->cqhp", c_blocks, entering, precision=HIGHEST)
        * jnp.exp(cumulative)[..., None]
    )
    return (within + across).reshape(length, head_count, head_width)


def gate_mix(signal, b_rows, c_rows, step_raw, gate_raw, head_local):
    length = signal.shape[0]
    head_count = head_local.shape[1]
    step_size = jax.nn.softplus(step_raw + head_local[1][None, :])
    shaped = signal.reshape(length, head_count, -1)
    mixed = (
        ssd_scan(shaped, b_rows, c_rows, step_size, head_local[0])
        + head_local[2][None, :, None] * shaped
    )
    return mixed.reshape(length, -1) * jax.nn.silu(gate_raw)


def gate_blocks(signal, b_rows, c_rows, step_raw, gate_raw, head_local):

    def one_sequence(element):
        return gate_mix(element[0], element[1], element[2], element[3], element[4], head_local)

    return lax.map(one_sequence, (signal, b_rows, c_rows, step_raw, gate_raw))


def conv_signal(values, params):
    return jax.vmap(causal_conv, (0, None, None))(values, params[:CONV], params[CONV])


def conv_state(values, params):
    return jax.vmap(causal_conv, (0, None, None))(values, params[:, :CONV].T, params[:, CONV])


def lamb_parts(weight, gradient, first_old, second_old):
    first_new = DECAY * first_old + (1.0 - DECAY) * gradient
    second_new = DECAY * second_old + (1.0 - DECAY) * gradient * gradient
    direction = (
        first_new / BIAS_FIRST / (jnp.sqrt(second_new / BIAS_SECOND) + ADAM_EPSILON)
        + WEIGHT_DECAY * weight
    )
    return (first_new, second_new, direction)


def local(
    block_input,
    output_grad,
    lengths,
    in_proj,
    step_proj,
    out_proj,
    channel_params,
    head_params,
    state_proj,
    state_conv,
    norm_gain,
    first_in_proj,
    first_step_proj,
    first_out_proj,
    first_channel_params,
    first_head_params,
    first_state_proj,
    first_state_conv,
    first_norm_gain,
    second_in_proj,
    second_step_proj,
    second_out_proj,
    second_channel_params,
    second_head_params,
    second_state_proj,
    second_state_conv,
    second_norm_gain,
):
    tensor_count = lax.axis_size("tensor")
    own_count = block_input.shape[0]
    group_count = own_count * tensor_count
    sequence_count = lengths.shape[0]
    by_sequence = (sequence_count, LMAX, -1)
    inputs = block_input.astype(jnp.float32)
    shared = (
        lax.all_gather(state_proj, ("dp", "tensor"), axis=0, tiled=True),
        lax.all_gather(state_conv, ("dp", "tensor"), axis=0, tiled=True),
        lax.all_gather(norm_gain, ("dp", "tensor"), axis=0, tiled=True),
    )
    state_weight = shared[0].astype(jnp.bfloat16)
    conv_whole = shared[1]
    gain_whole = shared[2]
    in_weight, step_weight, out_weight = (
        lax.all_gather(in_proj.astype(jnp.bfloat16), "dp", axis=0, tiled=True),
        lax.all_gather(step_proj.astype(jnp.bfloat16), "dp", axis=0, tiled=True),
        lax.all_gather(out_proj.astype(jnp.bfloat16), "dp", axis=0, tiled=True),
    )
    scale = lax.rsqrt(jnp.mean(inputs * inputs, axis=-1, keepdims=True) + EPSILON)
    normed_own = (inputs * scale * gain_whole[None, :]).astype(jnp.bfloat16)
    normed = lax.all_gather(normed_own, "tensor", axis=0, tiled=True)
    gate_raw = contract(normed, in_weight[:, 0, :], 1, 0)
    signal_raw = contract(normed, in_weight[:, 1, :], 1, 0)
    state_raw = contract(normed, state_weight, 1, 0)
    step_raw = contract(normed, step_weight, 1, 0)
    signal_act, signal_back = jax.vjp(
        conv_signal, signal_raw.reshape(by_sequence), channel_params[: CONV + 1]
    )
    state_act, state_back = jax.vjp(conv_state, state_raw.reshape(by_sequence), conv_whole)
    signal = rounded(signal_act)
    b_rows = rounded(state_act[:, :, :STATE])
    c_rows = rounded(state_act[:, :, STATE:])
    mixer_inputs = (
        signal,
        b_rows,
        c_rows,
        step_raw.reshape(by_sequence),
        gate_raw.reshape(by_sequence),
        head_params,
    )
    gated, mixer_back = jax.vjp(gate_blocks, *mixer_inputs)
    squares = lax.psum(jnp.sum(gated * gated, axis=-1), "tensor")
    gate_scale = lax.rsqrt(squares / INNER + EPSILON)[:, :, None]
    gate_gain = channel_params[CONV + 1]
    normalized = gated * gate_scale
    merged = (normalized * gate_gain).astype(jnp.bfloat16).reshape(group_count, -1)
    branch = lax.psum_scatter(
        contract(merged, out_weight, 1, 1), "tensor", scatter_dimension=0, tiled=True
    )
    position_all = lax.axis_index("tensor") * own_count + jnp.arange(own_count, dtype=jnp.int32)
    sequence_of = position_all // LMAX
    length_of = jnp.sum(
        jnp.where(
            sequence_of[:, None] == jnp.arange(sequence_count, dtype=jnp.int32)[None, :],
            lengths[None, :],
            0,
        ),
        axis=1,
    )
    live_own = (position_all % LMAX < length_of).astype(jnp.float32)[:, None]
    output = (inputs + branch * live_own).astype(jnp.bfloat16)
    masked_grad = jnp.where(live_own > 0.5, output_grad, jnp.zeros_like(output_grad))
    grad_rows = lax.all_gather(masked_grad, "tensor", axis=0, tiled=True)
    in_back, step_back, out_back = (
        lax.all_gather(in_proj.astype(jnp.bfloat16), "dp", axis=0, tiled=True),
        lax.all_gather(step_proj.astype(jnp.bfloat16), "dp", axis=0, tiled=True),
        lax.all_gather(out_proj.astype(jnp.bfloat16), "dp", axis=0, tiled=True),
    )
    merged_grad = contract(grad_rows, out_back, 1, 0).reshape(by_sequence)
    out_grad = contract(grad_rows, merged, 0, 0)
    weighted = merged_grad * gate_gain
    gain_grad = jnp.sum(merged_grad * normalized, axis=(0, 1))
    products = lax.psum(jnp.sum(weighted * gated, axis=-1), "tensor")
    gated_grad = gate_scale * weighted - gated * gate_scale**3 * (products / INNER)[:, :, None]
    signal_grad, b_grad, c_grad, step_grad, gate_grad, head_grad = mixer_back(gated_grad)
    signal_raw_grad, kernel_grad = signal_back(signal_grad)
    state_raw_grad, conv_grad = state_back(jnp.concatenate([b_grad, c_grad], axis=-1))
    gate_low = gate_grad.reshape(group_count, -1).astype(jnp.bfloat16)
    signal_low = signal_raw_grad.reshape(group_count, -1).astype(jnp.bfloat16)
    step_low = step_grad.reshape(group_count, -1).astype(jnp.bfloat16)
    in_grad = jnp.stack(
        [contract(normed, gate_low, 0, 0), contract(normed, signal_low, 0, 0)], axis=1
    )
    step_weight_grad = contract(normed, step_low, 0, 0)
    normed_part = (
        contract(gate_low, in_back[:, 0, :], 1, 1)
        + contract(signal_low, in_back[:, 1, :], 1, 1)
        + contract(step_low, step_back, 1, 1)
    )
    normed_sum, state_sum = (
        lax.psum_scatter(normed_part, "tensor", scatter_dimension=0, tiled=True),
        lax.psum_scatter(
            state_raw_grad.reshape(group_count, -1), "tensor", scatter_dimension=0, tiled=True
        ),
    )
    state_low = state_sum.astype(jnp.bfloat16)
    normed_grad = normed_sum + contract(state_low, state_weight, 1, 1)
    state_weight_grad = contract(normed_own, state_low, 0, 0)
    gain_in_grad = jnp.sum(normed_grad * inputs * scale, axis=0)
    scaled_grad = normed_grad * gain_whole[None, :]
    input_grad = (
        output_grad.astype(jnp.float32)
        + scale * scaled_grad
        - inputs * scale**3 * jnp.mean(scaled_grad * inputs, axis=-1, keepdims=True)
    )
    channel_grad = jnp.concatenate([kernel_grad, gain_grad[None, :]], axis=0)
    in_sum, step_sum, out_sum = (
        lax.psum_scatter(in_grad, "dp", scatter_dimension=0, tiled=True),
        lax.psum_scatter(step_weight_grad, "dp", scatter_dimension=0, tiled=True),
        lax.psum_scatter(out_grad, "dp", scatter_dimension=0, tiled=True),
    )
    channel_sum, head_sum = lax.psum((channel_grad, head_grad), "dp")
    state_proj_sum, state_conv_sum, gain_sum = (
        lax.psum_scatter(state_weight_grad, ("dp", "tensor"), scatter_dimension=0, tiled=True),
        lax.psum_scatter(conv_grad, ("dp", "tensor"), scatter_dimension=0, tiled=True),
        lax.psum_scatter(gain_in_grad, ("dp", "tensor"), scatter_dimension=0, tiled=True),
    )
    masters = (
        in_proj,
        step_proj,
        out_proj,
        channel_params,
        head_params,
        state_proj,
        state_conv,
        norm_gain,
    )
    gradients = (
        in_sum,
        step_sum,
        out_sum,
        channel_sum,
        head_sum,
        state_proj_sum,
        state_conv_sum,
        gain_sum,
    )
    firsts = (
        first_in_proj,
        first_step_proj,
        first_out_proj,
        first_channel_params,
        first_head_params,
        first_state_proj,
        first_state_conv,
        first_norm_gain,
    )
    seconds = (
        second_in_proj,
        second_step_proj,
        second_out_proj,
        second_channel_params,
        second_head_params,
        second_state_proj,
        second_state_conv,
        second_norm_gain,
    )
    dp_copies = float(lax.axis_size("dp"))
    copies = (1.0, 1.0, 1.0, dp_copies, dp_copies, 1.0, 1.0, 1.0)
    first_list = []
    second_list = []
    directions = []
    partials = []
    for weight, gradient, first_old, second_old, copy_count in zip(
        masters, gradients, firsts, seconds, copies
    ):
        first_new, second_new, direction = lamb_parts(weight, gradient, first_old, second_old)
        first_list.append(first_new)
        second_list.append(second_new)
        directions.append(direction)
        partials.append(
            jnp.stack(
                [jnp.sum(weight * weight) / copy_count, jnp.sum(direction * direction) / copy_count]
            )
        )
    norm_totals = lax.psum(jnp.stack(partials, axis=1), ("dp", "tensor"))
    lamb_norms = jnp.sqrt(norm_totals)
    update_list = [
        -RATE * lamb_norms[0, position] / lamb_norms[1, position] * directions[position]
        for position in range(8)
    ]
    return (
        output,
        input_grad,
        in_sum,
        step_sum,
        out_sum,
        channel_sum,
        head_sum,
        state_proj_sum,
        state_conv_sum,
        gain_sum,
        first_list[0],
        first_list[1],
        first_list[2],
        first_list[3],
        first_list[4],
        first_list[5],
        first_list[6],
        first_list[7],
        second_list[0],
        second_list[1],
        second_list[2],
        second_list[3],
        second_list[4],
        second_list[5],
        second_list[6],
        second_list[7],
        update_list[0],
        update_list[1],
        update_list[2],
        update_list[3],
        update_list[4],
        update_list[5],
        update_list[6],
        update_list[7],
        lamb_norms,
    )


def solution(mesh):
    placed = (
        P(("dp", "tensor"), None),
        P(("dp", "tensor"), None),
        P("dp"),
        P("dp", None, "tensor"),
        P("dp", "tensor"),
        P("dp", "tensor"),
        P(None, "tensor"),
        P(None, "tensor"),
        P(("dp", "tensor"), None),
        P(("dp", "tensor"), None),
        P(("dp", "tensor")),
        P("dp", None, "tensor"),
        P("dp", "tensor"),
        P("dp", "tensor"),
        P(None, "tensor"),
        P(None, "tensor"),
        P(("dp", "tensor"), None),
        P(("dp", "tensor"), None),
        P(("dp", "tensor")),
        P("dp", None, "tensor"),
        P("dp", "tensor"),
        P("dp", "tensor"),
        P(None, "tensor"),
        P(None, "tensor"),
        P(("dp", "tensor"), None),
        P(("dp", "tensor"), None),
        P(("dp", "tensor")),
    )
    return jax.shard_map(
        local,
        mesh=mesh,
        in_specs=placed,
        out_specs=(
            P(("dp", "tensor"), None),
            P(("dp", "tensor"), None),
            P("dp", None, "tensor"),
            P("dp", "tensor"),
            P("dp", "tensor"),
            P(None, "tensor"),
            P(None, "tensor"),
            P(("dp", "tensor"), None),
            P(("dp", "tensor"), None),
            P(("dp", "tensor")),
            P("dp", None, "tensor"),
            P("dp", "tensor"),
            P("dp", "tensor"),
            P(None, "tensor"),
            P(None, "tensor"),
            P(("dp", "tensor"), None),
            P(("dp", "tensor"), None),
            P(("dp", "tensor")),
            P("dp", None, "tensor"),
            P("dp", "tensor"),
            P("dp", "tensor"),
            P(None, "tensor"),
            P(None, "tensor"),
            P(("dp", "tensor"), None),
            P(("dp", "tensor"), None),
            P(("dp", "tensor")),
            P("dp", None, "tensor"),
            P("dp", "tensor"),
            P("dp", "tensor"),
            P(None, "tensor"),
            P(None, "tensor"),
            P(("dp", "tensor"), None),
            P(("dp", "tensor"), None),
            P(("dp", "tensor")),
            P(),
        ),
        check_vma=False,
    )
```

profile of v0, /device:TPU:0, one launch (start us, length us, event | category | flops | bytes accessed | tf_op | source)
XLA Modules:
  0.0 971.0 jit_solution(7439061539372715546)
XLA Ops:
  8.2 42.0 %all-reduce.26 = f32[768]{0:T(1024)S(1)} all-reduce(f32[768]{0:T(1024)S(1)} %dynamic-update-slice), channel_id=1, replica_groups=mesh['dp'=8,'tensor'=4] {'dp','tensor'}, use_global_device_ids=true, to_apply=%add.26 | all-reduce | flops 768 | bytes 6144
  57.8 40.9 %all_gather.27 = f32[256,5]{1,0:T(8,128)S(1)} all-gather(f32[8,5]{1,0:T(8,128)S(1)} %copy-done.72), channel_id=1, replica_groups=mesh['dp'=8,'tensor'=4] {'dp','tensor'}, dimensions={0}, use_global_device_ids=true | all-gather | bytes 5280 | tf_op jit(solution)/shard_map/all_gather | solution.py:146
  100.7 26.1 %all-gather = bf16[8,96,6]{1,2,0:T(8,128)(2,1)S(1)} all-gather(bf16[1,96,6]{1,2,0:T(8,128)(2,1)S(1)} %get-tuple-element.954), channel_id=1, replica_groups=mesh['dp'=8,'tensor'=4] {'dp'}, dimensions={0}, use_global_device_ids=true | all-gather | bytes 10368 | tf_op jit(solution)/shard_map/all_gather | solution.py:154
  128.2 40.5 %all_gather.30 = bf16[768,256]{1,0:T(8,128)(2,1)} all-gather(bf16[24,256]{1,0:T(8,128)(2,1)S(1)} %get-tuple-element.951), channel_id=1, replica_groups=mesh['dp'=8,'tensor'=4] {'dp','tensor'}, dimensions={0}, use_global_device_ids=true | all-gather | bytes 405504 | tf_op jit(solution)/shard_map/all_gather | solution.py:145
  206.3 18.3 %while.62 = (s32[]{:T(128)}, f32[6,64,128]{2,1,0:T(8,128)S(1)}, f32[8,6,64,128]{3,2,1,0:T(8,128)}, f32[8,6]{1,0:T(8,128)S(1)}, f32[8,6,1,1]{1,3,2,0:T(1,128)}, /...) while((s32[]{:T(128)}, f32[6,64,128]{2,1,0:T(8,128)S(1)}, ...), condition=%wide.region_4.5_spmd.clone, body=%wide.region_3.4_spmd.clone.sunk | while | flops 196611 | bytes 984808 | solution.py:63
  231.6 9.4 bitcast_add_fusion.3
  253.0 7.6 multiply_reduce_fusion.8
  260.6 7.8 psum.35
  274.3 60.4 %reduce-scatter.19.cloned.1.call-done = f32[96,384]{1,0:T(8,128)} async-done(((f32[768,384]{1,0:T(8,128)}), f32[96,384]{1,0:T(8,128)}) %reduce-scatter.19.cloned.1.call-update) | async-done | bytes 147472 | tf_op jit(solution)/shard_map/reduce_scatter | solution.py:248
  337.4 31.6 %all_gather.33 = bf16[768,384]{1,0:T(8,128)(2,1)S(1)} all-gather(bf16[96,384]{1,0:T(8,128)(2,1)S(1)} %get-tuple-element.940), channel_id=1, replica_groups=mesh['dp'=8,'tensor'=4] {'dp'}, dimensions={0}, use_global_device_ids=true | all-gather | bytes 663552 | tf_op jit(solution)/shard_map/all_gather | solution.py:155
  369.0 7.5 fusion.31
  376.5 6.6 psum.36
  409.9 16.4 %fusion.12 = (f32[8,256,6]{1,2,0:T(8,128)}, f32[8,256,6]{1,2,0:T(8,128)}, f32[8,256,6]{1,2,0:T(8,128)}, f32[8,256,256]{2,1,0:T(8,128)}) fusion(f32[8,256,6]{1,2,0:T(8,128)S(1)} %get-tuple-element.920, f32[8,256,6]{1,2,0:T(8,128)S(1)} %bitcast.370, f32[8,256,256]{2,1,0:T(8,128)S(1)} %copy-done.42, pred[256,256]{1,0:T(8,128)(4,1)S(1)} %copy-done.67, ...), kind=kOutput, calls=%fused_computation.24 | convolution fusion | flops 2456252416 | bytes 9224192 | tf_op jit(solution)/shard_map/transpose(jvp())/while/body/eval_jaxpr/cqkh,ckhp->cqhp/dot_general | solution.py:53
  436.9 26.4 %while.63 = (s32[]{:T(128)}, f32[6,64,128]{2,1,0:T(8,128)S(1)}, f32[8,6,64,128]{3,2,1,0:T(8,128)}, f32[8,6]{1,0:T(8,128)S(1)}, f32[8,6,64,128]{3,2,1,0:T(8,128)}...) while((s32[]{:T(128)}, f32[6,64,128]{2,1,0:T(8,128)S(1)}, ...), condition=%wide.region_12.13_spmd.clone, body=%wide.region_10.12_spmd.clone.sunk | while | flops 294916 | bytes 1180016 | solution.py:63
  463.3 8.4 fusion.69
  491.0 15.0 %reduce-window.28 = f32[8,6,2,128]{3,0,1,2:T(8,128)S(1)} reduce-window(f32[8,6,2,128]{3,0,1,2:T(8,128)S(1)} %copy.271, f32[]{:T(128)} %constant.337.clone.1), window={size=1x1x1x128 pad=0_0x0_0x0_0x0_127}, to_apply=%region_18.19 | reduce-window | flops 1560576 | bytes 98308 | tf_op jit(solution)/shard_map/reduce-window
  506.4 13.3 %bitcast_add_fusion.2 = f32[8,256,6,64]{1,3,2,0:T(8,128)S(1)} fusion(f32[8,256,6,64]{1,3,2,0:T(8,128)} %fusion.132, f32[8,256,6]{1,2,0:T(8,128)S(1)} %get-tuple-element.920, f32[8,256,6]{1,2,0:T(8,128)} %bitcast.368, f32[8,256,256]{2,1,0:T(8,128)} %copy-done.41, pred[256,256]{1,0:T(8,128)(4,1)} %iota_compare_fusion, f32[8,256,6,64]{1,3,2,0:T(8,128)} %copy-done.7, ...), kind=kOutput, calls=%fused_computation.57 | convolution fusion | flops 2430074880 | bytes 11747328 | tf_op jit(solution)/shard_map/transpose(jvp())/while/body/eval_jaxpr/cqkh,ckhp->cqhp/dot_general | solution.py:53
  534.6 11.2 %multiply_reduce_fusion.5 = (f32[384]{0:T(512)}, f32[384]{0:T(512)}, f32[384]{0:T(512)}, f32[384]{0:T(512)}, f32[384]{0:T(512)}, /*index=5*/f32[1,2048,384]{2,1,0:T(8,128)S(1)}) fusion(f32[1,2048,384]{2,1,0:T(8,128)} %bitcast.333, f32[2048,384]{1,0:T(8,128)} %copy-done.4, f32[1,2048,384]{2,1,0:T(8,128)} %get-tuple-element.918, f32[1,2048,384]{2,1,0:T(8,128)} %copy.264, ...), kind=kLoop, calls=%fused_computation.76 | loop fusion | flops 19658880 | bytes 22029312 | tf_op jit(solution)/shard_map/transpose(jvp(vmap()))/reduce_sum | solution.py:35
  591.3 35.5 %all-reduce.30 = (f32[6,384]{1,0:T(8,128)S(1)}, f32[3,6]{1,0:T(4,128)S(1)}) all-reduce(f32[6,384]{1,0:T(8,128)S(1)} %pad_maximum_fusion.2, f32[3,6]{1,0:T(4,128)S(1)} %pad_add_fusion.9), channel_id=1, replica_groups=mesh['dp'=8,'tensor'=4] {'dp'}, use_global_device_ids=true, to_apply=%region_33.34 | all-reduce | flops 2322 | bytes 18576 | tf_op jit(solution)/shard_map/psum | solution.py:250
  640.1 43.3 %reduce-scatter.17.cloned.1.call-done = f32[96,2,384]{2,0,1:T(8,128)} async-done(((f32[768,2,384]{2,0,1:T(8,128)}), f32[96,2,384]{2,0,1:T(8,128)}) %reduce-scatter.17.cloned.1.call-update) | async-done | bytes 294928 | tf_op jit(solution)/shard_map/reduce_scatter | solution.py:246
  689.9 94.7 %reduce-scatter.21.cloned.1.call-done = f32[24,256]{1,0:T(8,128)} async-done(((f32[768,256]{1,0:T(8,128)}), f32[24,256]{1,0:T(8,128)}) %reduce-scatter.21.cloned.1.call-update) | async-done | bytes 24592 | tf_op jit(solution)/shard_map/reduce_scatter | solution.py:252
  788.5 56.2 %reduce-scatter.13.cloned.1.call-done = f32[512,768]{1,0:T(8,128)} async-done(((f32[2048,768]{1,0:T(8,128)}), f32[512,768]{1,0:T(8,128)}) %reduce-scatter.13.cloned.1.call-update) | async-done | bytes 1572880 | tf_op jit(solution)/shard_map/reduce_scatter | solution.py:229
  847.6 39.9 %all-reduce.29 = (f32[256,5]{0,1:T(8,128)S(1)}, f32[768]{0:T(1024)S(1)}) all-reduce(f32[256,5]{0,1:T(8,128)} %pad_add_fusion.7, f32[768]{0:T(1024)} %get-tuple-element.823), channel_id=9, replica_groups=mesh['dp'=8,'tensor'=4] {'dp','tensor'}, use_global_device_ids=true, to_apply=%region_45.46.clone | all-reduce | flops 2048 | bytes 16384
  896.3 41.0 %psum.39 = f32[2,8]{1,0:T(2,128)S(1)} all-reduce(f32[2,8]{1,0:T(2,128)S(1)} %stack.143), channel_id=1, replica_groups=mesh['dp'=8,'tensor'=4] {'dp','tensor'}, use_global_device_ids=true, to_apply=%region_64.65 | all-reduce | flops 16 | bytes 128 | tf_op jit(solution)/shard_map/psum | solution.py:314
  (536 shorter events, 285.1 us)
Async XLA Ops:
  7.2 162.6 %all-gather.5.cloned.1.call-start = ((), (), s32[]{:S(2)}) async-start(), calls=%async_computation.7 | async-start | bytes 3932160 | tf_op jit(solution)/shard_map/all_gather | solution.py:159
  51.6 75.3 %copy-start.70 = (f32[6,384]{1,0:T(8,128)S(1)}, f32[6,384]{1,0:T(8,128)}, u32[]{:S(2)}) copy-start(f32[6,384]{1,0:T(8,128)} %param.37) | copy-start | bytes 27652
  51.6 76.0 %copy-start.63 = (f32[24,256]{1,0:T(8,128)S(1)}, f32[24,256]{1,0:T(8,128)}, u32[]{:S(2)}) copy-start(f32[24,256]{1,0:T(8,128)} %param.39) | copy-start | bytes 73732
  55.1 128.0 %all-gather.7.cloned.1.call-start = ((), (), s32[]{:S(2)}) async-start(), calls=%async_computation.8 | async-start | bytes 1327104 | tf_op jit(solution)/shard_map/all_gather | solution.py:153
  55.9 212.5 %all-gather.9.cloned.1.call-start = ((), (), s32[]{:S(2)}) async-start(), calls=%async_computation.10 | async-start | bytes 3932160 | tf_op jit(solution)/shard_map/all_gather | solution.py:201
  57.7 277.1 %reduce-scatter.19.cloned.1.call-start = ((), (), s32[]{:S(2)}) async-start(), calls=%async_computation.14 | async-start | bytes 1327104 | tf_op jit(solution)/shard_map/reduce_scatter | solution.py:248
  127.6 256.2 %copy-start.74 = (f32[384]{0:T(512)}, f32[384]{0:T(512)S(1)}, u32[]{:S(2)}) copy-start(f32[384]{0:T(512)S(1)} %get-tuple-element.831) | copy-start | bytes 4612
  169.8 83.2 %copy-start.79 = (f32[384]{0:T(512)}, f32[384]{0:T(512)S(1)}, u32[]{:S(2)}) copy-start(f32[384]{0:T(512)S(1)} %mul.1038) | copy-start | bytes 4612
  274.3 293.3 %reduce-scatter.15.cloned.1.call-start = ((), (), s32[]{:S(2)}) async-start(), calls=%async_computation.12 | async-start | bytes 2621440 | tf_op jit(solution)/shard_map/reduce_scatter | solution.py:230
  484.1 151.9 %reduce-scatter.23.cloned.1.call-start = ((), (), s32[]{:S(2)}) async-start(), calls=%async_computation.16 | async-start | bytes 442368
  550.6 132.9 %reduce-scatter.17.cloned.1.call-start = ((), (), s32[]{:S(2)}) async-start(), calls=%async_computation.13 | async-start | bytes 2654208 | tf_op jit(solution)/shard_map/reduce_scatter | solution.py:246
  561.7 222.9 %reduce-scatter.21.cloned.1.call-start = ((), (), s32[]{:S(2)}) async-start(), calls=%async_computation.15 | async-start | bytes 811008 | tf_op jit(solution)/shard_map/reduce_scatter | solution.py:252
  570.1 274.6 %reduce-scatter.13.cloned.1.call-start = ((), (), s32[]{:S(2)}) async-start(), calls=%async_computation.11 | async-start | bytes 7864320 | tf_op jit(solution)/shard_map/reduce_scatter | solution.py:229
  578.5 382.0 %reduce-scatter.11.cloned.1.call-start = ((), (), s32[]{:S(2)}) async-start(), calls=%async_computation.9 | async-start | bytes 7864320 | tf_op jit(solution)/shard_map/reduce_scatter | solution.py:185
  586.3 97.2 %copy-start.51 = (f32[96,2,384]{2,1,0:T(2,128)S(1)}, f32[96,2,384]{2,1,0:T(2,128)}, u32[]{:S(2)}) copy-start(f32[96,2,384]{2,1,0:T(2,128)} %param.50) | copy-start | bytes 884740
  586.3 97.2 %copy-start.52 = (f32[96,2,384]{2,1,0:T(2,128)S(1)}, f32[96,2,384]{2,1,0:T(2,128)}, u32[]{:S(2)}) copy-start(f32[96,2,384]{2,1,0:T(2,128)} %param.42) | copy-start | bytes 884740
  586.3 198.2 %copy-start.64 = (f32[24,256]{1,0:T(8,128)S(1)}, f32[24,256]{1,0:T(8,128)}, u32[]{:S(2)}) copy-start(f32[24,256]{1,0:T(8,128)} %param.39) | copy-start | bytes 73732
  586.3 198.2 %copy-start.77 = (f32[24,256]{1,0:T(8,128)S(1)}, f32[24,256]{1,0:T(8,128)}, u32[]{:S(2)}) copy-start(f32[24,256]{1,0:T(8,128)} %param.55) | copy-start | bytes 73732
  586.3 198.2 %copy-start.78 = (f32[24,256]{1,0:T(8,128)S(1)}, f32[24,256]{1,0:T(8,128)}, u32[]{:S(2)}) copy-start(f32[24,256]{1,0:T(8,128)} %param.47) | copy-start | bytes 73732
  586.3 258.3 %copy-start.27 = (bf16[512,768]{1,0:T(8,128)(2,1)S(1)}, bf16[512,768]{1,0:T(8,128)(2,1)}, u32[]{:S(2)}) copy-start(bf16[512,768]{1,0:T(8,128)(2,1)} %param.31) | copy-start | bytes 2359300
  586.4 258.3 %copy-start.35 = (bf16[768,256]{1,0:T(8,128)(2,1)S(1)}, bf16[768,256]{1,0:T(8,128)(2,1)}, u32[]{:S(2)}) copy-start(bf16[768,256]{1,0:T(8,128)(2,1)} %all_gather.30) | copy-start | bytes 1179652
  586.4 258.3 %copy-start.69 = (f32[768]{0:T(1024)S(1)}, f32[768]{0:T(1024)}, u32[]{:S(2)}) copy-start(f32[768]{0:T(1024)} %copy-done.68) | copy-start | bytes 9220
  636.9 151.7 %copy-start.91 = (f32[96,6]{0,1:T(8,128)}, f32[96,6]{0,1:T(8,128)S(1)}, u32[]{:S(2)}) copy-start(f32[96,6]{0,1:T(8,128)S(1)} %copy.311) | copy-start | bytes 6916
  788.5 172.0 %copy-start.37 = (bf16[512,768]{1,0:T(8,128)(2,1)S(1)}, bf16[512,768]{1,0:T(8,128)(2,1)}, u32[]{:S(2)}) copy-start(bf16[512,768]{1,0:T(8,128)(2,1)} %param.32) | copy-start | bytes 2359300
  (118 other events, 1623.9 us)
Sparse Core Ops, SparseCore 0:
  55.2 29.0 all-gather.4
  87.1 41.1 all-gather.6
  129.8 29.2 all-gather.8
  274.4 60.3 reduce-scatter.18
  484.2 30.5 reduce-scatter.14
  550.7 60.5 reduce-scatter.22
  615.2 68.1 reduce-scatter.16
  689.9 94.5 reduce-scatter.20
  787.2 57.4 reduce-scatter.12
  847.1 59.2 reduce-scatter.10
where the time goes:
time: 977 us; the launch traced here: 971 us
  blocking collectives  312 us (32%)
  waiting for transfers between devices  255 us (26%)
  other arithmetic  155 us (16%)
  matrix products  125 us (13%)
  local copies, waits for them, and re-layouts  92.9 us (10%)
  between operations  29.8 us (3%)
    reduce_scatter x1, waiting for transfers between devices, local(): lax.psum_scatter(state_weight_grad, ('dp', 'tensor'), scatter_dimension=0...  94.7 us
    unnamed x2, blocking collectives  81.9 us
    reduce_scatter x1, waiting for transfers between devices, local(): lax.psum_scatter(out_grad, 'dp', scatter_dimension=0, tiled=True)  60.4 us
    reduce_scatter x1, waiting for transfers between devices, local(): lax.psum_scatter(normed_part, 'tensor', scatter_dimension=0, tiled=True)  56.2 us
    dot_general x14, matrix products, contract(): lax.dot_general(left, right, (((left_dim,), (right_dim,)), ((), ())), pre...  55 us
    reduce_scatter x1, waiting for transfers between devices, local(): lax.psum_scatter(in_grad, 'dp', scatter_dimension=0, tiled=True)  43.3 us
    psum x1, blocking collectives, local(): norm_totals = lax.psum(jnp.stack(partials, axis=1), ('dp', 'tensor'))  41 us
    all_gather x1, blocking collectives, local(): lax.all_gather(state_conv, ('dp', 'tensor'), axis=0, tiled=True)  40.9 us
  transfers between devices with their start and end apart: 10, of which 4 were waited for; matrix products, arithmetic and copies ran while one was open for 25% of the time, Pallas kernels for 0%

commit v1 on v0

--- a/solution.py
+++ b/solution.py
@@ -16,6 +16,19 @@
 RATE = 0.3
 WEIGHT_DECAY = 0.01
 HIGHEST = lax.Precision.HIGHEST
+
+
+def gather_around(value, axis, dim):
+    ways = lax.axis_size(axis)
+    up = [(d, (d + 1) % ways) for d in range(ways)]
+    down = [(d, (d - 1) % ways) for d in range(ways)]
+    earlier, later = ([value], [value])
+    for _ in range(ways // 2):
+        earlier.append(lax.ppermute(earlier[-1], axis, up))
+    for _ in range((ways - 1) // 2):
+        later.append(lax.ppermute(later[-1], axis, down))
+    line = jnp.concatenate([*earlier[::-1], *later[1:]], axis=dim)
+    return jnp.roll(line, (lax.axis_index(axis) - ways // 2) * value.shape[dim], axis=dim)
 
 
 def rounded(values):
@@ -152,7 +165,7 @@
     in_weight, step_weight, out_weight = (
         lax.all_gather(in_proj.astype(jnp.bfloat16), "dp", axis=0, tiled=True),
         lax.all_gather(step_proj.astype(jnp.bfloat16), "dp", axis=0, tiled=True),
-        lax.all_gather(out_proj.astype(jnp.bfloat16), "dp", axis=0, tiled=True),
+        gather_around(out_proj.astype(jnp.bfloat16), "dp", 0),
     )
     scale = lax.rsqrt(jnp.mean(inputs * inputs, axis=-1, keepdims=True) + EPSILON)
     normed_own = (inputs * scale * gain_whole[None, :]).astype(jnp.bfloat16)

time: 977 us -> 985 us (level)
  starting transfers between devices: 0.42 us -> 14.9 us
  waiting for transfers between devices: 255 us -> 241 us
  local copies, waits for them, and re-layouts: 92.9 us -> 105 us
    reduce_scatter x1, waiting for transfers between devices: 43.3 us -> 14.3 us  [local(): lax.psum_scatter(in_grad, 'dp', scatter_dimension=0, tiled=True)]
    ppermute x0 -> x7, starting transfers between devices: none -> 14.5 us  [the longest x3 14.4 us: gather_around(): later.append(lax.ppermute(later[-1], axis, down))]
    ppermute x0 -> x7, waiting for transfers between devices: none -> 13.7 us  [the longest x4 13.7 us: gather_around(): earlier.append(lax.ppermute(earlier[-1], axis, up))]
    dynamic_update_slice x24, local copies, waits for them, and re-layouts: 4.67 us -> 14.8 us  [ssd_scan(): unused, entering = lax.scan(carry_step, initial, (states, closing))]
    unnamed x286 -> x291, local copies, waits for them, and re-layouts: 30.9 us -> 35 us
  transfers between devices with their start and end apart: 10 -> 17, of which waited for: 4 -> 8; matrix products, arithmetic and copies ran while one was open for 25% -> 25% of each run, Pallas kernels for 0% -> 0%
where the time goes in v1:
time: 985 us; the launch traced here: 979 us
  blocking collectives  310 us (31%)
  waiting for transfers between devices  241 us (24%)
  other arithmetic  153 us (16%)
  matrix products  125 us (13%)
  local copies, waits for them, and re-layouts  105 us (11%)
  between operations  29.9 us (3%)
  starting transfers between devices  14.9 us (2%)
    reduce_scatter x1, waiting for transfers between devices, local(): lax.psum_scatter(state_weight_grad, ('dp', 'tensor'), scatter_dimension=0...  95.9 us
    unnamed x2, blocking collectives  81.8 us
    reduce_scatter x1, waiting for transfers between devices, local(): lax.psum_scatter(out_grad, 'dp', scatter_dimension=0, tiled=True)  59.8 us
    reduce_scatter x1, waiting for transfers between devices, local(): lax.psum_scatter(normed_part, 'tensor', scatter_dimension=0, tiled=True)  56.8 us
    dot_general x14, matrix products, contract(): lax.dot_general(left, right, (((left_dim,), (right_dim,)), ((), ())), pre...  55.4 us
    psum x1, blocking collectives, local(): norm_totals = lax.psum(jnp.stack(partials, axis=1), ('dp', 'tensor'))  41.1 us
    all_gather x1, blocking collectives, local(): lax.all_gather(state_conv, ('dp', 'tensor'), axis=0, tiled=True)  40.9 us
    all_gather x1, blocking collectives, local(): lax.all_gather(state_proj, ('dp', 'tensor'), axis=0, tiled=True)  40.5 us
  transfers between devices with their start and end apart: 17, of which 8 were waited for; matrix products, arithmetic and copies ran while one was open for 25% of the time, Pallas kernels for 0%

profile of v1, /device:TPU:0, one launch (start us, length us, event | category | flops | bytes accessed | tf_op | source)
XLA Modules:
  0.0 979.2 jit_solution(16307056527182655911)
XLA Ops:
  8.2 42.0 %all-reduce.26 = f32[768]{0:T(1024)S(1)} all-reduce(f32[768]{0:T(1024)S(1)} %dynamic-update-slice), channel_id=1, replica_groups=mesh['dp'=8,'tensor'=4] {'dp','tensor'}, use_global_device_ids=true, to_apply=%add.26 | all-reduce | flops 768 | bytes 6144
  57.2 40.9 %all_gather.26 = f32[256,5]{1,0:T(8,128)S(1)} all-gather(f32[8,5]{1,0:T(8,128)S(1)} %copy-done.66), channel_id=1, replica_groups=mesh['dp'=8,'tensor'=4] {'dp','tensor'}, dimensions={0}, use_global_device_ids=true | all-gather | bytes 5280 | tf_op jit(solution)/shard_map/all_gather | solution.py:159
  100.1 26.1 %all-gather = bf16[8,96,6]{1,2,0:T(8,128)(2,1)S(1)} all-gather(bf16[1,96,6]{1,2,0:T(8,128)(2,1)S(1)} %get-tuple-element.954), channel_id=1, replica_groups=mesh['dp'=8,'tensor'=4] {'dp'}, dimensions={0}, use_global_device_ids=true | all-gather | bytes 10368 | tf_op jit(solution)/shard_map/all_gather | solution.py:167
  127.6 40.5 %all_gather.29 = bf16[768,256]{1,0:T(8,128)(2,1)} all-gather(bf16[24,256]{1,0:T(8,128)(2,1)S(1)} %get-tuple-element.951), channel_id=1, replica_groups=mesh['dp'=8,'tensor'=4] {'dp','tensor'}, dimensions={0}, use_global_device_ids=true | all-gather | bytes 405504 | tf_op jit(solution)/shard_map/all_gather | solution.py:158
  206.1 18.3 %while.62 = (s32[]{:T(128)}, f32[6,64,128]{2,1,0:T(8,128)S(1)}, f32[8,6,64,128]{3,2,1,0:T(8,128)}, f32[8,6]{1,0:T(8,128)S(1)}, f32[8,6,1,1]{1,3,2,0:T(1,128)}, /...) while((s32[]{:T(128)}, f32[6,64,128]{2,1,0:T(8,128)S(1)}, ...), condition=%wide.region_4.5_spmd.clone, body=%wide.region_3.4_spmd.clone.sunk | while | flops 196611 | bytes 984808 | solution.py:76
  231.4 9.4 bitcast_add_fusion.3
  252.7 7.7 multiply_reduce_fusion.8
  260.3 7.8 psum.35
  274.7 59.8 %reduce-scatter.19.cloned.1.call-done = f32[96,384]{1,0:T(8,128)} async-done(((f32[768,384]{1,0:T(8,128)}), f32[96,384]{1,0:T(8,128)}) %reduce-scatter.19.cloned.1.call-update) | async-done | bytes 147472 | tf_op jit(solution)/shard_map/reduce_scatter | solution.py:261
  337.2 31.6 %all_gather.33 = bf16[768,384]{1,0:T(8,128)(2,1)S(1)} all-gather(bf16[96,384]{1,0:T(8,128)(2,1)S(1)} %get-tuple-element.940), channel_id=1, replica_groups=mesh['dp'=8,'tensor'=4] {'dp'}, dimensions={0}, use_global_device_ids=true | all-gather | bytes 663552 | tf_op jit(solution)/shard_map/all_gather | solution.py:218
  368.8 7.3 fusion.31
  409.5 16.4 %fusion.12 = (f32[8,256,6]{1,2,0:T(8,128)}, f32[8,256,6]{1,2,0:T(8,128)}, f32[8,256,6]{1,2,0:T(8,128)}, f32[8,256,256]{2,1,0:T(8,128)}) fusion(f32[8,256,6]{1,2,0:T(8,128)S(1)} %get-tuple-element.920, f32[8,256,6]{1,2,0:T(8,128)S(1)} %bitcast.369, f32[8,256,256]{2,1,0:T(8,128)S(1)} %copy-done.40, pred[256,256]{1,0:T(8,128)(4,1)S(1)} %copy-done.61, ...), kind=kOutput, calls=%fused_computation.24 | convolution fusion | flops 2456252416 | bytes 9224192 | tf_op jit(solution)/shard_map/transpose(jvp())/while/body/eval_jaxpr/cqkh,ckhp->cqhp/dot_general | solution.py:66
  437.1 40.5 %while.63 = (s32[]{:T(128)}, f32[6,64,128]{2,1,0:T(8,128)S(1)}, f32[8,6,64,128]{3,2,1,0:T(8,128)}, f32[8,6]{1,0:T(8,128)}, f32[8,6,64,128]{3,2,1,0:T(8,128)}, /*...) while((s32[]{:T(128)}, f32[6,64,128]{2,1,0:T(8,128)S(1)}, ...), condition=%wide.region_12.13_spmd.clone, body=%wide.region_10.12_spmd.clone.sunk | while | flops 294916 | bytes 1180016 | solution.py:76
  477.6 8.4 fusion.69
  505.3 15.0 %reduce-window.28 = f32[8,6,2,128]{3,0,1,2:T(8,128)S(1)} reduce-window(f32[8,6,2,128]{3,0,1,2:T(8,128)S(1)} %copy.271, f32[]{:T(128)} %constant.359.clone.1), window={size=1x1x1x128 pad=0_0x0_0x0_0x0_127}, to_apply=%region_18.19 | reduce-window | flops 1560576 | bytes 98308 | tf_op jit(solution)/shard_map/reduce-window
  520.7 13.4 %bitcast_add_fusion.2 = f32[8,256,6,64]{1,3,2,0:T(8,128)S(1)} fusion(f32[8,256,6,64]{1,3,2,0:T(8,128)} %fusion.134, f32[8,256,6]{1,2,0:T(8,128)S(1)} %get-tuple-element.920, f32[8,256,6]{1,2,0:T(8,128)} %bitcast.367, f32[8,256,256]{2,1,0:T(8,128)} %copy-done.39, pred[256,256]{1,0:T(8,128)(4,1)} %iota_compare_fusion, f32[8,256,6,64]{1,3,2,0:T(8,128)} %copy-done.7, ...), kind=kOutput, calls=%fused_computation.57 | convolution fusion | flops 2430074880 | bytes 11747328 | tf_op jit(solution)/shard_map/transpose(jvp())/while/body/eval_jaxpr/cqkh,ckhp->cqhp/dot_general | solution.py:66
  548.4 11.0 %multiply_reduce_fusion.5 = (f32[384]{0:T(512)S(1)}, f32[384]{0:T(512)S(1)}, f32[384]{0:T(512)S(1)}, f32[384]{0:T(512)S(1)}, f32[384]{0:T(512)S(1)}, /*index=5*/f32[1,2048,384]{2,1,0:T(8,128)S(1)}) fusion(f32[1,2048,384]{2,1,0:T(8,128)} %bitcast.332, f32[2048,384]{1,0:T(8,128)} %copy-done.4, f32[1,2048,384]{2,1,0:T(8,128)} %get-tuple-element.918, ...), kind=kLoop, calls=%fused_computation.76 | loop fusion | flops 19658880 | bytes 22029312 | tf_op jit(solution)/shard_map/transpose(jvp(vmap()))/reduce_sum | solution.py:48
  594.4 7.1 collective-permute-done
  639.8 34.0 %all-reduce.30 = (f32[6,384]{1,0:T(8,128)S(1)}, f32[3,6]{1,0:T(4,128)S(1)}) all-reduce(f32[6,384]{1,0:T(8,128)S(1)} %pad_maximum_fusion.2, f32[3,6]{1,0:T(4,128)S(1)} %pad_add_fusion.9), channel_id=1, replica_groups=mesh['dp'=8,'tensor'=4] {'dp'}, use_global_device_ids=true, to_apply=%region_33.34 | all-reduce | flops 2322 | bytes 18576 | tf_op jit(solution)/shard_map/psum | solution.py:263
  684.3 14.3 %reduce-scatter.17.cloned.1.call-done = f32[96,2,384]{2,0,1:T(8,128)} async-done(((f32[768,2,384]{2,0,1:T(8,128)}), f32[96,2,384]{2,0,1:T(8,128)}) %reduce-scatter.17.cloned.1.call-update) | async-done | bytes 294928 | tf_op jit(solution)/shard_map/reduce_scatter | solution.py:259
  703.8 95.9 %reduce-scatter.21.cloned.1.call-done = f32[24,256]{1,0:T(8,128)} async-done(((f32[768,256]{1,0:T(8,128)}), f32[24,256]{1,0:T(8,128)}) %reduce-scatter.21.cloned.1.call-update) | async-done | bytes 24592 | tf_op jit(solution)/shard_map/reduce_scatter | solution.py:265
  803.1 56.8 %reduce-scatter.13.cloned.1.call-done = f32[512,768]{1,0:T(8,128)} async-done(((f32[2048,768]{1,0:T(8,128)}), f32[512,768]{1,0:T(8,128)}) %reduce-scatter.13.cloned.1.call-update) | async-done | bytes 1572880 | tf_op jit(solution)/shard_map/reduce_scatter | solution.py:242
  862.2 39.8 %all-reduce.29 = (f32[256,5]{0,1:T(8,128)S(1)}, f32[768]{0:T(1024)S(1)}) all-reduce(f32[256,5]{0,1:T(8,128)S(1)} %pad_add_fusion.7, f32[768]{0:T(1024)S(1)} %get-tuple-element.823), channel_id=9, replica_groups=mesh['dp'=8,'tensor'=4] {'dp','tensor'}, use_global_device_ids=true, to_apply=%region_45.46.clone | all-reduce | flops 2048 | bytes 16384
  907.9 41.1 %psum.39 = f32[2,8]{1,0:T(2,128)S(1)} all-reduce(f32[2,8]{1,0:T(2,128)S(1)} %stack.143), channel_id=1, replica_groups=mesh['dp'=8,'tensor'=4] {'dp','tensor'}, use_global_device_ids=true, to_apply=%region_64.65 | all-reduce | flops 16 | bytes 128 | tf_op jit(solution)/shard_map/psum | solution.py:327
  (556 shorter events, 322.4 us)
Async XLA Ops:
  7.2 162.5 %all-gather.5.cloned.1.call-start = ((), (), s32[]{:S(2)}) async-start(), calls=%async_computation.7 | async-start | bytes 3932160 | tf_op jit(solution)/shard_map/all_gather | solution.py:172
  54.5 128.4 %all-gather.7.cloned.1.call-start = ((), (), s32[]{:S(2)}) async-start(), calls=%async_computation.8 | async-start | bytes 1327104 | tf_op jit(solution)/shard_map/all_gather | solution.py:166
  55.3 212.9 %all-gather.9.cloned.1.call-start = ((), (), s32[]{:S(2)}) async-start(), calls=%async_computation.10 | async-start | bytes 3932160 | tf_op jit(solution)/shard_map/all_gather | solution.py:214
  57.1 277.4 %reduce-scatter.19.cloned.1.call-start = ((), (), s32[]{:S(2)}) async-start(), calls=%async_computation.14 | async-start | bytes 1327104 | tf_op jit(solution)/shard_map/reduce_scatter | solution.py:261
  274.0 308.3 %reduce-scatter.15.cloned.1.call-start = ((), (), s32[]{:S(2)}) async-start(), calls=%async_computation.12 | async-start | bytes 2621440 | tf_op jit(solution)/shard_map/reduce_scatter | solution.py:243
  498.4 182.3 %reduce-scatter.23.cloned.1.call-start = ((), (), s32[]{:S(2)}) async-start(), calls=%async_computation.16 | async-start | bytes 442368
  564.3 134.4 %reduce-scatter.17.cloned.1.call-start = ((), (), s32[]{:S(2)}) async-start(), calls=%async_computation.13 | async-start | bytes 2654208 | tf_op jit(solution)/shard_map/reduce_scatter | solution.py:259
  575.4 224.3 %reduce-scatter.21.cloned.1.call-start = ((), (), s32[]{:S(2)}) async-start(), calls=%async_computation.15 | async-start | bytes 811008 | tf_op jit(solution)/shard_map/reduce_scatter | solution.py:265
  584.8 275.1 %reduce-scatter.13.cloned.1.call-start = ((), (), s32[]{:S(2)}) async-start(), calls=%async_computation.11 | async-start | bytes 7864320 | tf_op jit(solution)/shard_map/reduce_scatter | solution.py:242
  594.3 374.1 %reduce-scatter.11.cloned.1.call-start = ((), (), s32[]{:S(2)}) async-start(), calls=%async_computation.9 | async-start | bytes 7864320 | tf_op jit(solution)/shard_map/reduce_scatter | solution.py:198
  594.3 7.1 collective-permute-start
  601.5 7.0 collective-permute-start.1
  601.5 7.1 collective-permute-start.4
  608.5 7.2 collective-permute-start.2
  609.1 6.6 collective-permute-start.5
  615.7 7.5 collective-permute-start.3
  615.7 12.0 %collective-permute-start.6 = (bf16[96,384]{1,0:T(8,128)(2,1)}, bf16[96,384]{1,0:T(8,128)(2,1)S(1)}, u32[]{:S(2)}, u32[]{:S(2)}) collective-permute-start(bf16[96,384]{1,0:T(8,128)(2,1)} %collective-permute-done.5), channel_id=1, source_target_pairs={{0,28},{4,0},{8,4},{12,8},{16,12},{20,16},{24,20},{28,24},{1,29},{... | collective-permute-start | bytes 221192 | tf_op jit(solution)/shard_map/ppermute | solution.py:29
  637.2 222.7 %copy-start.27 = (bf16[512,768]{1,0:T(8,128)(2,1)S(1)}, bf16[512,768]{1,0:T(8,128)(2,1)}, u32[]{:S(2)}) copy-start(bf16[512,768]{1,0:T(8,128)(2,1)} %param.31) | copy-start | bytes 2359300
  637.2 222.7 %copy-start.35 = (bf16[768,256]{1,0:T(8,128)(2,1)S(1)}, bf16[768,256]{1,0:T(8,128)(2,1)}, u32[]{:S(2)}) copy-start(bf16[768,256]{1,0:T(8,128)(2,1)} %all_gather.29) | copy-start | bytes 1179652
  637.2 222.7 %copy-start.63 = (f32[768]{0:T(1024)S(1)}, f32[768]{0:T(1024)}, u32[]{:S(2)}) copy-start(f32[768]{0:T(1024)} %copy-done.62) | copy-start | bytes 9220
  637.2 222.7 %copy-start.69 = (f32[512]{0:T(512)S(1)}, f32[512]{0:T(512)}, u32[]{:S(2)}) copy-start(f32[512]{0:T(512)} %copy-done.68) | copy-start | bytes 6148
  700.4 201.6 %copy-start.125 = (f32[24]{0:T(128)S(1)}, f32[24]{0:T(128)}, u32[]{:S(2)}) copy-start(f32[24]{0:T(128)} %param.57) | copy-start | bytes 292
  700.4 201.6 %copy-start.126 = (f32[24]{0:T(128)S(1)}, f32[24]{0:T(128)}, u32[]{:S(2)}) copy-start(f32[24]{0:T(128)} %param.49) | copy-start | bytes 292
  701.9 205.0 %copy-start.41 = (f32[96,2,384]{2,0,1:T(8,128)S(1)}, f32[96,2,384]{2,0,1:T(8,128)}, u32[]{:S(2)}) copy-start(f32[96,2,384]{2,0,1:T(8,128)} %reduce-scatter.17.cloned.1.call-done) | copy-start | bytes 884740
  (120 other events, 3183.3 us)
Sparse Core Ops, SparseCore 0:
  54.6 29.0 all-gather.4
  86.5 41.1 all-gather.6
  129.2 29.2 all-gather.8
  274.2 60.3 reduce-scatter.18
  498.5 30.5 reduce-scatter.14
  564.4 61.3 reduce-scatter.22
  629.6 68.9 reduce-scatter.16
  705.1 94.5 reduce-scatter.20
  802.4 57.4 reduce-scatter.12
  862.3 59.5 reduce-scatter.10
